TPU v7x, 32 devices: a whole 2x2x4 slice. The times are simulated.
32 devices in a mesh: grp: 8 (over z, x), lane: 4 (over y, core).
Axes of the slice: x: 2, y: 2, z: 4, core: 2. Of those that a mesh axis runs over, the one named last changes fastest.
Arguments:
- features: bfloat16 [65536, 128], P(('grp', 'lane')), may hold values from -600 to 600
- tiles: bfloat16 [512, 7, 128, 128], P(('grp', 'lane')), may hold values from -0.125 to 0.125
- tile_cols: int32 [512, 7], P(('grp', 'lane')), may hold values from 0 to 23
- send_index: int32 [32, 2, 512], P(('grp', 'lane')), may hold values from 0 to 2047
- send_count: int32 [32, 2], P(('grp', 'lane')), may hold values from 128 to 512, as said below
- coef: float32 [4, 128], replicated, may hold values from -1 to 1
- dest_lane: int32 [65536], P(('grp', 'lane')), may hold values from 0 to 3, as said below
- dest_slot: int32 [65536], P(('grp', 'lane')), may hold values from 0 to 2047, as said below
Outputs:
- table_out: bfloat16 [65536, 128], P(('grp', 'lane'))
Inputs may be any that keep to these rules, and one draw needn't show every extreme that they name: `send_count`: in every draw for each of the two directions some partition has exactly 512 live rows towards that neighbour. `dest_lane`: within each relayout group every row of every table shard is named by exactly one node; at most 1024 rows of one partition go to one shard, and exactly 1024 for some pair in every group. `dest_slot`: together with dest_lane, a one-to-one map of a group's nodes onto its table rows.
All inputs are finite; a program needn't handle non-finite values.
Results may differ from a plain program's by a relative error of at most 0.008.
Values may be sent and summed in bfloat16 or wider, within the bound.
A program may use at most 64 MiB of HBM per device.

v0:
```python
import jax
import jax.numpy as jnp
from jax import lax
from jax.sharding import PartitionSpec as P

ORDER = 3


def from_behind(value, axis, by):
    devices = lax.axis_size(axis)
    return lax.ppermute(value, axis, [(i, (i + by) % devices) for i in range(devices)])


def to_ball(white, feature_width):
    norms = jnp.sqrt(jnp.sum(white * white, axis=1, keepdims=True) + 1e-06)
    radius = jnp.sqrt(jnp.float32(feature_width))
    return (jnp.tanh(norms / radius) * radius * white / norms).astype(jnp.bfloat16)


def whiten(values, factor, node_total):
    solved = jax.scipy.linalg.solve_triangular(factor, values.T, lower=True).T
    return solved * jnp.sqrt(jnp.float32(node_total))


def pack_rows(values, destination, slot_ids, lanes, capacity):
    row_count = values.shape[0]
    onehot = (destination[:, None] == jnp.arange(lanes)[None, :]).astype(jnp.int32)
    rank_in_run = jnp.sum(jnp.cumsum(onehot, axis=0) * onehot, axis=1) - 1
    position = destination * capacity + rank_in_run
    buffer = jnp.zeros((lanes * capacity, values.shape[1]), values.dtype).at[position].set(values)
    slot_buffer = jnp.full((lanes * capacity,), row_count, jnp.int32).at[position].set(slot_ids)
    return (buffer.reshape(lanes, capacity, values.shape[1]), slot_buffer.reshape(lanes, capacity))


def place_rows(received, received_slots, row_count):
    flat_slots = received_slots.reshape(-1)
    empty = jnp.zeros((row_count, received.shape[-1]), jnp.bfloat16)
    return empty.at[flat_slots].set(received, mode="drop")


def body(features, tiles, tile_cols, send_index, send_count, coef, dest_lane, dest_slot):
    row_count, feature_width = features.shape
    tile_size = tiles.shape[2]
    lanes = lax.axis_size("lane")
    node_total = row_count * lax.axis_size("grp") * lanes
    capacity = 2 * row_count // lanes
    boundary = send_index.shape[2]
    valid_rows = jnp.arange(boundary)[None, :] < send_count[0][:, None]

    def operate(current):
        upward = jnp.where(
            valid_rows[0][:, None], current[send_index[0, 0]], jnp.zeros((), jnp.bfloat16)
        )
        downward = jnp.where(
            valid_rows[1][:, None], current[send_index[0, 1]], jnp.zeros((), jnp.bfloat16)
        )
        from_lower = from_behind(upward, "grp", 1)
        from_upper = from_behind(downward, "grp", -1)
        extended = jnp.concatenate([current, from_lower, from_upper], axis=0).reshape(
            -1, tile_size, feature_width
        )
        blocks = extended[tile_cols]
        product = jnp.einsum("bkij,bkjf->bif", tiles, blocks, preferred_element_type=jnp.float32)
        return product.reshape(row_count, feature_width)

    def next_term(cheb_terms):
        if len(cheb_terms) == 1:
            return operate(cheb_terms[0]).astype(jnp.bfloat16)
        return (2.0 * operate(cheb_terms[-1]) - cheb_terms[-2].astype(jnp.float32)).astype(
            jnp.bfloat16
        )

    cheb_terms = [features]
    for term_order in range(1, ORDER):
        cheb_terms.append(next_term(cheb_terms))
    cheb_terms.append(next_term(cheb_terms))
    mixed = jnp.zeros((row_count, feature_width), jnp.float32)
    for term_order in range(ORDER + 1):
        mixed = mixed + coef[term_order][None, :] * cheb_terms[term_order].astype(jnp.float32)
    raw_buffer, raw_slots = pack_rows(mixed, dest_lane, dest_slot, lanes, capacity)
    received_raw, received_slots = (
        lax.all_to_all(raw_buffer, "lane", split_axis=0, concat_axis=0, tiled=True),
        lax.all_to_all(raw_slots, "lane", split_axis=0, concat_axis=0, tiled=True),
    )
    local_gram = jnp.einsum("rf,rg->fg", mixed, mixed, precision=lax.Precision.HIGHEST)
    gram = lax.psum(local_gram, ("grp", "lane"))
    factor = jnp.linalg.cholesky(gram)
    flat_raw = received_raw.reshape(-1, feature_width)
    ball_rows = to_ball(whiten(flat_raw, factor, node_total), feature_width)
    return place_rows(ball_rows, received_slots, row_count)


def solution(mesh):
    placed = (
        P(("grp", "lane"), None),
        P(("grp", "lane"), None, None, None),
        P(("grp", "lane"), None),
        P(("grp", "lane"), None, None),
        P(("grp", "lane"), None),
        P(),
        P(("grp", "lane")),
        P(("grp", "lane")),
    )
    return jax.shard_map(
        body, mesh=mesh, in_specs=placed, out_specs=P(("grp", "lane"), None), check_vma=False
    )
```

profile of v0, /device:TPU:0, one launch (start us, length us, event | category | flops | bytes accessed | tf_op | source)
XLA Modules:
  0.0 244.3 jit_solution(8330663186755694221)
XLA Ops:
  6.5 0.8 compare_select_fusion.3
  7.3 0.7 iota_compare_fusion.4
  8.1 2.2 gather_fusion
  10.2 0.1 broadcast_select_fusion.5
  10.4 3.0 %collective-permute-start = (bf16[512,128]{1,0:T(8,128)(2,1)S(1)}, bf16[512,128]{1,0:T(8,128)(2,1)S(1)}, u32[]{:S(2)}, u32[]{:S(2)}) collective-permute-start(bf16[512,128]{1,0:T(8,128)(2,1)S(1)} %broadcast_select_fusion.5), channel_id=1, source_target_pairs={{0,4},{4,8},{8,12},{12,16},{16,20},{20,24},{24,28},{28,0},{1,5},{5... | collective-permute-start | bytes 393224 | tf_op jit(solution)/shard_map/ppermute | solution.py:11
  13.4 1.3 gather_fusion.1
  14.7 0.1 broadcast_select_fusion.2
  14.9 3.1 %collective-permute-start.1 = (bf16[512,128]{1,0:T(8,128)(2,1)S(1)}, bf16[512,128]{1,0:T(8,128)(2,1)S(1)}, u32[]{:S(2)}, u32[]{:S(2)}) collective-permute-start(bf16[512,128]{1,0:T(8,128)(2,1)S(1)} %broadcast_select_fusion.2), channel_id=1, source_target_pairs={{0,28},{4,0},{8,4},{12,8},{16,12},{20,16},{24,20},{28,24},{1,29},{... | collective-permute-start | bytes 393224 | tf_op jit(solution)/shard_map/ppermute | solution.py:11
  18.0 0.1 copy.12
  18.1 0.1 reshape.183
  18.2 1.2 reduce-window.6
  19.4 0.2 slice_reduce_fusion
  19.6 0.2 reduce-window.9
  19.8 0.1 add_bitcast_fusion
  19.9 0.1 collective-permute-done
  20.0 2.7 %collective-permute-done.1 = bf16[512,128]{1,0:T(8,128)(2,1)S(1)} collective-permute-done((bf16[512,128]{1,0:T(8,128)(2,1)S(1)}, bf16[512,128]{1,0:T(8,128)(2,1)S(1)}, u32[]{:S(2)}, u32[]{:S(2)}) %collective-permute-start.1) | collective-permute-done | bytes 131104 | tf_op jit(solution)/shard_map/ppermute | solution.py:11
  22.7 0.1 pad_maximum_fusion
  22.8 2.9 %gather_fusion.2 = bf16[112,128,128]{2,1,0:T(8,128)(2,1)} fusion(bf16[24,128,128]{2,1,0:T(8,128)(2,1)S(1)} %bitcast.98, s32[1024]{0:T(1024)S(1)} %pad_clamp_fusion), kind=kCustom, calls=%fused_computation.2 | custom fusion | bytes 7340480 | tf_op jit(solution)/shard_map/gather | solution.py:62
  25.6 4.3 %fusion.2 = bf16[16,128,128]{1,2,0:T(8,128)(2,1)S(1)} fusion(bf16[16,7,128,128]{3,2,1,0:T(8,128)(2,1)} %param.9, bf16[16,7,128,128]{3,2,1,0:T(8,128)(2,1)} %bitcast.94), kind=kOutput, calls=%fused_computation.23 | convolution fusion | flops 470024192 | bytes 7864320 | tf_op jit(solution)/shard_map/bkij,bkjf->bif/dot_general | solution.py:63
  29.9 1.3 gather_fusion.3
  31.2 1.3 gather_fusion.4
  32.6 0.1 broadcast_select_fusion.4
  32.7 0.1 collective-permute-start.2
  32.8 0.1 broadcast_select_fusion.1
  32.9 4.8 %collective-permute-start.3 = (bf16[512,128]{1,0:T(8,128)(2,1)S(1)}, bf16[512,128]{1,0:T(8,128)(2,1)S(1)}, u32[]{:S(2)}, u32[]{:S(2)}) collective-permute-start(bf16[512,128]{1,0:T(8,128)(2,1)S(1)} %broadcast_select_fusion.1), channel_id=1, source_target_pairs={{0,28},{4,0},{8,4},{12,8},{16,12},{20,16},{24,20},{28,24},{1,29},{... | collective-permute-start | bytes 393224 | tf_op jit(solution)/shard_map/ppermute | solution.py:11
  37.7 8.8 %scatter_custom_fusion = s32[4096]{0:T(1024)} fusion(s32[2048]{0:T(1024)S(1)} %compare_select_fusion.1, s32[2048]{0:T(1024)} %param.15, s32[]{:T(128)} %constant.66.clone.1), kind=kCustom, calls=%fused_computation.66 | custom fusion | bytes 16896 | tf_op jit(solution)/shard_map/scatter | solution.py:31
  46.5 3.2 %all-to-all-start = ((s32[4,1,1024]{2,1,0:T(1,128)}), s32[4,1,1024]{2,1,0:T(1,128)S(1)}, u32[]{:S(2)}, u32[]{:S(2)}) async-start(s32[4,1,1024]{2,1,0:T(1,128)} %bitcast.2), calls=%async_computation | async-start | bytes 32768 | tf_op jit(solution)/shard_map/all_to_all | solution.py:83
  49.7 0.0 all-reduce.2.cloned.1.call-start
  49.8 0.0 collective-permute-done.2
  49.8 0.0 collective-permute-done.3
  49.8 0.1 pad_maximum_fusion.1
  49.9 2.9 %gather_fusion.5 = bf16[112,128,128]{2,1,0:T(8,128)(2,1)} fusion(bf16[24,128,128]{2,1,0:T(8,128)(2,1)S(1)} %bitcast.99, s32[1024]{0:T(1024)S(1)} %pad_clamp_fusion), kind=kCustom, calls=%fused_computation.5 | custom fusion | bytes 7340480 | tf_op jit(solution)/shard_map/gather | solution.py:62
  52.7 4.3 %fusion = f32[16,128,128]{1,2,0:T(8,128)S(1)} fusion(bf16[16,7,128,128]{3,2,1,0:T(8,128)(2,1)} %param.9, bf16[16,7,128,128]{3,2,1,0:T(8,128)(2,1)} %bitcast.96), kind=kOutput, calls=%fused_computation.17 | convolution fusion | flops 470024192 | bytes 8388608 | tf_op jit(solution)/shard_map/bkij,bkjf->bif/dot_general | solution.py:63
  57.0 0.0 copy-start.3
  57.0 0.1 fusion.6
  57.1 1.3 gather_fusion.6
  58.5 1.3 gather_fusion.7
  59.8 0.1 broadcast_select_fusion.3
  60.0 0.1 collective-permute-start.4
  60.0 0.1 broadcast_select_fusion
  60.2 4.9 %collective-permute-start.5 = (bf16[512,128]{1,0:T(8,128)(2,1)S(1)}, bf16[512,128]{1,0:T(8,128)(2,1)S(1)}, u32[]{:S(2)}, u32[]{:S(2)}) collective-permute-start(bf16[512,128]{1,0:T(8,128)(2,1)S(1)} %broadcast_select_fusion), channel_id=1, source_target_pairs={{0,28},{4,0},{8,4},{12,8},{16,12},{20,16},{24,20},{28,24},{1,29},{... | collective-permute-start | bytes 393224 | tf_op jit(solution)/shard_map/ppermute | solution.py:11
  65.1 3.5 %collective-permute-done.4 = bf16[512,128]{1,0:T(8,128)(2,1)S(1)} collective-permute-done((bf16[512,128]{1,0:T(8,128)(2,1)S(1)}, bf16[512,128]{1,0:T(8,128)(2,1)S(1)}, u32[]{:S(2)}, u32[]{:S(2)}) %collective-permute-start.4) | collective-permute-done | bytes 131104 | tf_op jit(solution)/shard_map/ppermute | solution.py:11
  68.7 0.4 collective-permute-done.5
  69.1 0.1 pad_maximum_fusion.2
  69.1 2.9 %gather_fusion.8 = bf16[112,128,128]{2,1,0:T(8,128)(2,1)} fusion(bf16[24,128,128]{2,1,0:T(8,128)(2,1)S(1)} %bitcast.97, s32[1024]{0:T(1024)S(1)} %pad_clamp_fusion), kind=kCustom, calls=%fused_computation.8 | custom fusion | bytes 7340480 | tf_op jit(solution)/shard_map/gather | solution.py:62
  72.0 4.3 %fusion.1 = f32[16,128,128]{1,2,0:T(8,128)S(1)} fusion(bf16[16,7,128,128]{3,2,1,0:T(8,128)(2,1)} %param.9, bf16[16,7,128,128]{3,2,1,0:T(8,128)(2,1)} %bitcast.95), kind=kOutput, calls=%fused_computation.18 | convolution fusion | flops 470024192 | bytes 8388608 | tf_op jit(solution)/shard_map/bkij,bkjf->bif/dot_general | solution.py:63
  76.3 0.4 fusion.5
  76.7 2.4 %fusion.21 = f32[128,128]{0,1:T(8,128)} fusion(f32[2048,128]{1,0:T(8,128)S(1)} %fusion.5), kind=kOutput, calls=%fused_computation.79 | convolution fusion | flops 402653184 | bytes 1114112 | tf_op jit(solution)/shard_map/rf,rg->fg/dot_general | solution.py:85
  79.2 0.0 all-reduce.2.cloned.1.call-update
  79.2 7.0 %scatter_custom_fusion.1 = f32[4096,128]{1,0:T(8,128)} fusion(s32[2048]{0:T(1024)S(1)} %compare_select_fusion.1, f32[2048,128]{1,0:T(8,128)S(1)} %fusion.5, f32[]{:T(128)} %constant.71.clone.1), kind=kCustom, calls=%fused_computation.29 | custom fusion | bytes 2097156 | tf_op jit(solution)/shard_map/scatter | solution.py:30
  86.2 0.0 all-to-all-done
  86.2 3.8 %all-to-all-start.1 = ((f32[4,1024,128]{2,1,0:T(8,128)}), f32[4,1024,128]{2,1,0:T(8,128)S(1)}, u32[]{:S(2)}, u32[]{:S(2)}) async-start(f32[4,1024,128]{2,1,0:T(8,128)} %bitcast.100), calls=%async_computation.1 | async-start | bytes 4194304 | tf_op jit(solution)/shard_map/all_to_all | solution.py:82
  90.1 108.0 %all-reduce.2.cloned.1.call-done = f32[128,128]{0,1:T(8,128)} async-done(((f32[128,128]{0,1:T(8,128)}), f32[128,128]{0,1:T(8,128)}) %all-reduce.2.cloned.1.call-update) | async-done | bytes 65552 | tf_op jit(solution)/shard_map/psum | solution.py:86
  198.1 0.9 copy.14
  199.0 0.9 fusion.15
  199.9 11.7 %cholesky.16 = f32[128,128]{1,0:T(8,128)S(1)} custom-call(f32[128,128]{1,0:T(8,128)S(1)} %fusion.15), custom_call_target="Cholesky" | custom-call | tf_op jit(solution)/shard_map/jit(cholesky)/cholesky | solution.py:87
  211.7 0.6 compare_reduce_fusion
  212.3 0.7 fusion.12
  213.0 9.8 %custom-call.7 = f32[1,128,128]{1,2,0:T(8,128)S(1)} custom-call(f32[1,128,128]{2,1,0:T(8,128)S(1)} %fusion.12), custom_call_target="InvertDiagBlocksLowerTriangular" | custom-call | tf_op jit(solution)/shard_map/jit(_solve_triangular)/triangular_solve | solution.py:21
  222.8 0.0 all-to-all-done.1
  222.8 2.2 multiply_reduce_fusion
  225.0 0.2 divide_convert_fusion
  225.2 0.7 copy.15
  225.9 11.6 %scatter_custom_fusion.2 = bf16[2048,128]{1,0:T(8,128)(2,1)} fusion(s32[4096]{0:T(1024)S(1)} %bitcast.104, bf16[4096,128]{1,0:T(8,128)(2,1)S(1)} %copy.15, bf16[]{:T(256)} %constant.65.clone.1), kind=kCustom, calls=%fused_computation.34 | custom fusion | bytes 524290 | tf_op jit(solution)/shard_map/scatter | solution.py:38
  (19 shorter events, 0.2 us)
Async XLA Ops:
  6.5 6.9 %copy-start = (bf16[2048,128]{1,0:T(8,128)(2,1)S(1)}, bf16[2048,128]{1,0:T(8,128)(2,1)}, u32[]{:S(2)}) copy-start(bf16[2048,128]{1,0:T(8,128)(2,1)} %param.8) | copy-start | bytes 1572868
  6.5 11.5 %copy-start.2 = (s32[16,7]{0,1:T(8,128)S(1)}, s32[16,7]{0,1:T(8,128)}, u32[]{:S(2)}) copy-start(s32[16,7]{0,1:T(8,128)} %param.10) | copy-start | bytes 1348
  6.5 11.6 %copy-start.1 = (s32[2048]{0:T(1024)S(1)}, s32[2048]{0:T(1024)}, u32[]{:S(2)}) copy-start(s32[2048]{0:T(1024)} %param.14) | copy-start | bytes 24580
  10.4 9.6 %collective-permute-start = (bf16[512,128]{1,0:T(8,128)(2,1)S(1)}, bf16[512,128]{1,0:T(8,128)(2,1)S(1)}, u32[]{:S(2)}, u32[]{:S(2)}) collective-permute-start(bf16[512,128]{1,0:T(8,128)(2,1)S(1)} %broadcast_select_fusion.5), channel_id=1, source_target_pairs={{0,4},{4,8},{8,12},{12,16},{16,20},{20,24},{24,28},{28,0},{1,5},{5... | collective-permute-start | bytes 393224 | tf_op jit(solution)/shard_map/ppermute | solution.py:11
  14.9 7.8 %collective-permute-start.1 = (bf16[512,128]{1,0:T(8,128)(2,1)S(1)}, bf16[512,128]{1,0:T(8,128)(2,1)S(1)}, u32[]{:S(2)}, u32[]{:S(2)}) collective-permute-start(bf16[512,128]{1,0:T(8,128)(2,1)S(1)} %broadcast_select_fusion.2), channel_id=1, source_target_pairs={{0,28},{4,0},{8,4},{12,8},{16,12},{20,16},{24,20},{28,24},{1,29},{... | collective-permute-start | bytes 393224 | tf_op jit(solution)/shard_map/ppermute | solution.py:11
  32.7 17.0 %collective-permute-start.2 = (bf16[512,128]{1,0:T(8,128)(2,1)S(1)}, bf16[512,128]{1,0:T(8,128)(2,1)S(1)}, u32[]{:S(2)}, u32[]{:S(2)}) collective-permute-start(bf16[512,128]{1,0:T(8,128)(2,1)S(1)} %broadcast_select_fusion.4), channel_id=1, source_target_pairs={{0,4},{4,8},{8,12},{12,16},{16,20},{20,24},{24,28},{28,0},{1,5},{5... | collective-permute-start | bytes 393224 | tf_op jit(solution)/shard_map/ppermute | solution.py:11
  32.9 16.8 %collective-permute-start.3 = (bf16[512,128]{1,0:T(8,128)(2,1)S(1)}, bf16[512,128]{1,0:T(8,128)(2,1)S(1)}, u32[]{:S(2)}, u32[]{:S(2)}) collective-permute-start(bf16[512,128]{1,0:T(8,128)(2,1)S(1)} %broadcast_select_fusion.1), channel_id=1, source_target_pairs={{0,28},{4,0},{8,4},{12,8},{16,12},{20,16},{24,20},{28,24},{1,29},{... | collective-permute-start | bytes 393224 | tf_op jit(solution)/shard_map/ppermute | solution.py:11
  46.5 39.7 %all-to-all-start = ((s32[4,1,1024]{2,1,0:T(1,128)}), s32[4,1,1024]{2,1,0:T(1,128)S(1)}, u32[]{:S(2)}, u32[]{:S(2)}) async-start(s32[4,1,1024]{2,1,0:T(1,128)} %bitcast.2), calls=%async_computation | async-start | bytes 32768 | tf_op jit(solution)/shard_map/all_to_all | solution.py:83
  49.7 148.4 %all-reduce.2.cloned.1.call-start = ((), (), s32[]{:S(2)}) async-start(), calls=%async_computation.2 | async-start | bytes 131072 | tf_op jit(solution)/shard_map/psum | solution.py:86
  57.0 8.1 %copy-start.3 = (f32[4,128]{1,0:T(4,128)S(1)}, f32[4,128]{1,0:T(4,128)}, u32[]{:S(2)}) copy-start(f32[4,128]{1,0:T(4,128)} %param.13) | copy-start | bytes 6148
  60.0 8.7 %collective-permute-start.4 = (bf16[512,128]{1,0:T(8,128)(2,1)S(1)}, bf16[512,128]{1,0:T(8,128)(2,1)S(1)}, u32[]{:S(2)}, u32[]{:S(2)}) collective-permute-start(bf16[512,128]{1,0:T(8,128)(2,1)S(1)} %broadcast_select_fusion.3), channel_id=1, source_target_pairs={{0,4},{4,8},{8,12},{12,16},{16,20},{20,24},{24,28},{28,0},{1,5},{5... | collective-permute-start | bytes 393224 | tf_op jit(solution)/shard_map/ppermute | solution.py:11
  60.2 8.9 %collective-permute-start.5 = (bf16[512,128]{1,0:T(8,128)(2,1)S(1)}, bf16[512,128]{1,0:T(8,128)(2,1)S(1)}, u32[]{:S(2)}, u32[]{:S(2)}) collective-permute-start(bf16[512,128]{1,0:T(8,128)(2,1)S(1)} %broadcast_select_fusion), channel_id=1, source_target_pairs={{0,28},{4,0},{8,4},{12,8},{16,12},{20,16},{24,20},{28,24},{1,29},{... | collective-permute-start | bytes 393224 | tf_op jit(solution)/shard_map/ppermute | solution.py:11
  86.2 136.6 %all-to-all-start.1 = ((f32[4,1024,128]{2,1,0:T(8,128)}), f32[4,1024,128]{2,1,0:T(8,128)S(1)}, u32[]{:S(2)}, u32[]{:S(2)}) async-start(f32[4,1024,128]{2,1,0:T(8,128)} %bitcast.100), calls=%async_computation.1 | async-start | bytes 4194304 | tf_op jit(solution)/shard_map/all_to_all | solution.py:82
Sparse Core Ops, SparseCore 0:
  79.3 118.7 all-reduce.1
where the time goes:
time: 246 us; the launch traced here: 244 us
  waiting for transfers between devices  115 us (47%)
  local copies, waits for them, and re-layouts  46.9 us (19%)
  other arithmetic  28.5 us (12%)
  starting transfers between devices  23 us (9%)
  matrix products  17.4 us (7%)
  between operations  13.7 us (6%)
    psum x1, waiting for transfers between devices, body(): gram = lax.psum(local_gram, ('grp', 'lane'))  108 us
    ppermute x6, starting transfers between devices, from_behind(): lax.ppermute(value, axis, [(i, (i + by) % devices) for i in range(devices)])  15.9 us
    dot_general x3, matrix products, operate(): jnp.einsum('bkij,bkjf->bif', tiles, blocks, preferred_element_type=jnp.fl...  12.8 us
    another operation x3, other arithmetic, body(): factor = jnp.linalg.cholesky(gram)  12.4 us
    scatter x1, local copies, waits for them, and re-layouts, place_rows(): return empty.at[flat_slots].set(received, mode='drop')  11.6 us
    another operation x2, other arithmetic, whiten(): solved = jax.scipy.linalg.solve_triangular(factor, values.T, lower=True).T  10.5 us
    scatter x1, local copies, waits for them, and re-layouts, pack_rows(): jnp.full((lanes * capacity,), row_count, jnp.int32).at[position]  8.78 us
    gather x3, local copies, waits for them, and re-layouts, operate(): blocks = extended[tile_cols]  8.6 us
  transfers between devices with their start and end apart: 9, of which 5 were waited for; matrix products, arithmetic and copies ran while one was open for 26% of the time, Pallas kernels for 0%

commit v1 on v0

v1 whole, which is shorter than its diff:
```python
import functools
import math

import jax
import jax.numpy as jnp
from jax import lax
from jax.experimental import pallas as pl
from jax.experimental.pallas import tpu as pltpu
from jax.sharding import PartitionSpec as P

MESH = pl.DeviceIdType.MESH
BF = jnp.bfloat16
F32 = jnp.float32
ORDER = 3
SUB = 8


def onehot(flags):
    return jnp.where(flags, 1.0, 0.0).astype(BF)


def eliminate(gram, node_total):
    size = gram.shape[0]
    blocks = size // SUB
    sub = lax.broadcasted_iota(jnp.int32, (SUB, size), 0)
    lane = lax.broadcasted_iota(jnp.int32, (SUB, size), 1)
    left = [gram[i * SUB : (i + 1) * SUB, :] for i in range(blocks)]
    right = [jnp.where(lane == sub + i * SUB, 1.0, 0.0).astype(F32) for i in range(blocks)]
    for j in range(size):
        own, row = divmod(j, SUB)
        pivot_row = left[own][row : row + 1, :]
        pivot_right = right[own][row : row + 1, :]
        inverse = 1.0 / pivot_row[:, j : j + 1]
        scaled = pivot_row * inverse
        scaled_right = pivot_right * inverse
        for i in range(own, blocks):
            column = left[i][:, j : j + 1]
            if i == own:
                column = jnp.where(sub[:, :1] > row, column, 0.0)
            left[i] = left[i] - column * scaled
            right[i] = right[i] - column * scaled_right
    root = math.sqrt(node_total)
    result = []
    for i in range(blocks):
        pivots = jnp.sum(jnp.where(lane == sub + i * SUB, left[i], 0.0), axis=1, keepdims=True)
        result.append(right[i] * (root / jnp.sqrt(pivots)))
    return jnp.concatenate(result, axis=0)


def kernel(
    groups, lanes, cols, counts, feats, tiles, index, coef, dest_lane, dest_slot, out,
    ext0, ext1, ext2, tile_v, pick, snd, mixed, low, gat, codes, part, rs_buf, lane_buf, chunk, tot, placed,
    load_sem, halo_s, halo_r, code_s, code_r, rs_s, rs_r, ln_s, ln_r, ag_s, ag_r, x_s, x_r, f_s, f_r,
):
    g, l = lax.axis_index("grp"), lax.axis_index("lane")
    own_blocks, tile, width = feats.shape
    rows = own_blocks * tile
    ext = (ext0, ext1, ext2)
    per_block = tiles.shape[1]
    bnd = index.shape[1]
    lists = bnd // tile
    node_total = rows * groups * lanes
    half = lanes // 2
    sibling = l + 1 - 2 * lax.rem(l, 2)

    def grp_at(t):
        return (lax.rem(g + t + groups, groups), l)

    def lane_at(t):
        return (g, lax.rem(l + t + lanes, lanes))

    load_tiles = pltpu.make_async_copy(tiles, tile_v, load_sem.at[0])
    load_feats = pltpu.make_async_copy(feats, ext[0].at[pl.ds(0, own_blocks)], load_sem.at[1])
    load_feats.start()
    load_tiles.start()

    barrier = pltpu.get_barrier_semaphore()
    for t in range(1, groups):
        pl.semaphore_signal(barrier, inc=1, device_id=grp_at(t), device_id_type=MESH)
    for t in range(1, lanes):
        pl.semaphore_signal(barrier, inc=1, device_id=lane_at(t), device_id_type=MESH)

    codes[0] = dest_lane[...] * rows + dest_slot[...]

    row_pos = lax.broadcasted_iota(jnp.int32, (tile, tile), 0)
    lane_pos = lax.broadcasted_iota(jnp.int32, (tile, tile), 1)
    for d in range(2):
        for c in range(bnd // tile):
            wanted = jnp.broadcast_to(index[d : d + 1, c * tile : (c + 1) * tile], (tile, tile)).T
            wanted = jnp.where(row_pos + c * tile < counts[0, d], wanted, -1)
            for r in range(rows // tile):
                pick[pl.ds(d * bnd + c * tile, tile), pl.ds(r * tile, tile)] = onehot(
                    wanted == lane_pos + r * tile
                )

    load_feats.wait()
    pl.semaphore_wait(barrier, groups - 1 + lanes - 1)

    def remote(src, dst, s, r, device):
        return pltpu.make_async_remote_copy(
            src_ref=src, dst_ref=dst, send_sem=s, recv_sem=r, device_id=device, device_id_type=MESH
        )

    def halo(k):
        copies = []
        for d in range(2):
            def gather(c, _, d=d):
                at = pl.multiple_of(d * bnd + c * 256, 256)
                picked = jnp.dot(
                    pick[pl.ds(at, 256), :], ext[k][pl.ds(0, own_blocks)].reshape(rows, width),
                    preferred_element_type=F32
                ).astype(BF)
                for part_at in range(256 // tile):
                    snd[k, (d * bnd + c * 256) // tile + part_at] = picked[
                        part_at * tile : (part_at + 1) * tile
                    ]
                return 0
            lax.fori_loop(0, bnd // 256, gather, 0)
            copy = remote(
                snd.at[k, pl.ds(d * lists, lists)], ext[k].at[pl.ds(own_blocks + d * lists, lists)],
                halo_s.at[k, d], halo_r.at[k, d], grp_at(1 - 2 * d),
            )
            copy.start()
            copies.append(copy)
        return copies

    halo_copies = halo(0)
    code_copies = []
    for t in range(1, lanes):
        copy = remote(codes.at[0], codes.at[t], code_s.at[t], code_r.at[t], lane_at(t))
        copy.start()
        code_copies.append(copy)
    load_tiles.wait()

    for k in range(1, ORDER + 1):
        for copy in halo_copies:
            copy.wait()

        def block(b, _, k=k):
            at = pl.ds(pl.multiple_of(b * tile, tile), tile)
            lhs = jnp.concatenate([tile_v[b, j] for j in range(per_block)], axis=1)
            rhs = jnp.concatenate(
                [
                    ext[k - 1][cols[b, j]]
                    for j in range(per_block)
                ],
                axis=0,
            )
            value = jnp.dot(lhs, rhs, preferred_element_type=F32)
            if k > 1:
                value = 2.0 * value - ext[k - 2][b].astype(F32)
            term = value.astype(BF)
            if k == 1:
                total = coef[0:1, :] * ext[0][b].astype(F32)
            else:
                total = mixed[at]
            total = total + coef[k : k + 1, :] * term.astype(F32)
            if k < ORDER:
                ext[k][b] = term
                mixed[at] = total
            else:
                high = total.astype(BF)
                gat[0, at] = high
                low[at] = (total - high.astype(F32)).astype(BF)
            return 0

        lax.fori_loop(0, rows // tile, block, 0, unroll=4)
        if k < ORDER:
            halo_copies = halo(k)

    step = 512
    square = jnp.zeros((2 * width, 2 * width), F32)
    for c in range(rows // step):
        both = jnp.concatenate([gat[0, pl.ds(c * step, step)], low[pl.ds(c * step, step)]], axis=1)
        square = square + lax.dot_general(
            both, both, (((0,), (0,)), ((), ())), preferred_element_type=F32
        )
    own_gram = (square[:width, :width] + square[width:, width:]) + (
        square[:width, width:] + square[width:, :width]
    )
    share = width // groups
    for t in range(groups):
        part[t] = own_gram[t * share : (t + 1) * share, :]

    rs_copies = []
    for t in range(1, groups):
        peer = grp_at(t)
        copy = remote(part.at[peer[0]], rs_buf.at[t], rs_s.at[t], rs_r.at[t], peer)
        copy.start()
        rs_copies.append(copy)
    sib_copies = [remote(gat.at[0], gat.at[half], f_s.at[0], f_r.at[0], (g, sibling))]
    sib_copies[0].start()
    for copy in code_copies:
        copy.wait()

    def place(gat_slot, code_slot, first):
        tall = 256

        def body(c, _):
            at = pl.ds(pl.multiple_of(c * tall, tall), tall)
            target = lax.broadcasted_iota(jnp.int32, (tall, tile), 0) + (c * tall + l * rows)
            selector = jnp.concatenate(
                [onehot(codes[code_slot, r : r + 1, :] == target) for r in range(rows // tile)], axis=1
            )
            value = jnp.dot(selector, gat[gat_slot], preferred_element_type=F32).astype(BF)
            if first:
                placed[at] = value
            else:
                placed[at] = placed[at] + value
            return 0

        lax.fori_loop(0, rows // tall, body, 0)

    for copy in rs_copies:
        copy.wait()
    summed = part[g]
    for t in range(1, groups):
        summed = summed + rs_buf[t]
    lane_buf[0] = summed
    ln_copies = []
    for t in range(1, lanes):
        copy = remote(lane_buf.at[0], lane_buf.at[t], ln_s.at[t], ln_r.at[t], lane_at(t))
        copy.start()
        ln_copies.append(copy)
    x_copies = [None]
    for t in range(1, half):
        copy = remote(gat.at[0], gat.at[t], x_s.at[t], x_r.at[t], lane_at(2 * t))
        copy.start()
        x_copies.append(copy)
    for copy in ln_copies:
        copy.wait()
    total_chunk = lane_buf[0]
    for t in range(1, lanes):
        total_chunk = total_chunk + lane_buf[t]
    chunk[...] = total_chunk
    tot[0] = total_chunk
    ag_copies = []
    for t in range(1, groups):
        copy = remote(chunk, tot.at[t], ag_s.at[t], ag_r.at[t], grp_at(t))
        copy.start()
        ag_copies.append(copy)
    place(0, 0, True)
    for copy in ag_copies:
        copy.wait()
    gram = jnp.concatenate(
        [tot[lax.rem(g - r + groups, groups)] for r in range(groups)], axis=0
    )
    whitener = eliminate(gram, node_total)
    high = whitener.astype(BF)
    rhs = jnp.concatenate([high, (whitener - high.astype(F32)).astype(BF)], axis=0)

    for t in range(1, half):
        x_copies[t].wait()
        copy = remote(gat.at[t], gat.at[half + t], f_s.at[t], f_r.at[t], (g, sibling))
        copy.start()
        sib_copies.append(copy)
    for t in range(1, half):
        place(t, 2 * t, False)
    for t in range(half):
        sib_copies[t].wait()
        place(half + t, lax.rem(l - sibling + 2 * t + lanes, lanes), False)

    radius = math.sqrt(width)

    def ball(c, _):
        at = pl.ds(pl.multiple_of(c * 256, 256), 256)
        pair = lax.dot_general(
            placed[at], rhs, (((1,), (1,)), ((), ())), preferred_element_type=F32
        )
        white = pair[:, :width] + pair[:, width:]
        norms = jnp.sqrt(jnp.sum(white * white, axis=1, keepdims=True) + 1e-06)
        out[at] = (white * (jnp.tanh(norms / radius) * radius / norms)).astype(BF)
        return 0

    lax.fori_loop(0, rows // 256, ball, 0)


def body(features, tiles, tile_cols, send_index, send_count, coef, dest_lane, dest_slot):
    groups, lanes = lax.axis_size("grp"), lax.axis_size("lane")
    rows, width = features.shape
    blocks, per_block, tile, _ = tiles.shape
    bnd = send_index.shape[2]
    half = lanes // 2
    share = width // groups
    dma = pltpu.SemaphoreType.DMA
    vmem = pl.BlockSpec(memory_space=pltpu.VMEM)
    smem = pl.BlockSpec(memory_space=pltpu.SMEM)
    hbm = pl.BlockSpec(memory_space=pl.ANY)
    return pl.pallas_call(
        functools.partial(kernel, groups, lanes),
        out_shape=jax.ShapeDtypeStruct((rows, width), BF),
        in_specs=[smem, smem, hbm, hbm, vmem, vmem, vmem, vmem],
        out_specs=vmem,
        scratch_shapes=[
            *[pltpu.VMEM(((rows + 2 * bnd) // tile, tile, width), BF)] * ORDER,
            pltpu.VMEM((blocks, per_block, tile, tile), BF),
            pltpu.VMEM((2 * bnd, rows), BF),
            pltpu.VMEM((ORDER, 2 * bnd // tile, tile, width), BF),
            pltpu.VMEM((rows, width), F32),
            pltpu.VMEM((rows, width), BF),
            pltpu.VMEM((lanes, rows, width), BF),
            pltpu.VMEM((lanes, rows // 128, 128), jnp.int32),
            pltpu.VMEM((groups, share, width), F32),
            pltpu.VMEM((groups, share, width), F32),
            pltpu.VMEM((lanes, share, width), F32),
            pltpu.VMEM((share, width), F32),
            pltpu.VMEM((groups, share, width), F32),
            pltpu.VMEM((rows, width), BF),
            dma((2,)),
            dma((ORDER, 2)), dma((ORDER, 2)),
            dma((lanes,)), dma((lanes,)),
            dma((groups,)), dma((groups,)),
            dma((lanes,)), dma((lanes,)),
            dma((groups,)), dma((groups,)),
            dma((half,)), dma((half,)),
            dma((half,)), dma((half,)),
        ],
        compiler_params=pltpu.CompilerParams(
            collective_id=0, has_side_effects=True, vmem_limit_bytes=52 * 1024 * 1024
        ),
    )(
        tile_cols, send_count, features.reshape(-1, tile, width), tiles, send_index.reshape(2, bnd), coef,
        dest_lane.reshape(-1, 128), dest_slot.reshape(-1, 128),
    )


def solution(mesh):
    placed = (
        P(("grp", "lane"), None),
        P(("grp", "lane"), None, None, None),
        P(("grp", "lane"), None),
        P(("grp", "lane"), None, None),
        P(("grp", "lane"), None),
        P(),
        P(("grp", "lane")),
        P(("grp", "lane")),
    )
    return jax.shard_map(
        body, mesh=mesh, in_specs=placed, out_specs=P(("grp", "lane"), None), check_vma=False
    )
```

time: 246 us -> 79.5 us (0.32)
  waiting for transfers between devices: 115 us -> 0 us
  Pallas kernels: 0 us -> 73.1 us
  local copies, waits for them, and re-layouts: 46.9 us -> 6.01 us
  other arithmetic: 28.5 us -> 0 us
  starting transfers between devices: 23 us -> 0 us
  matrix products: 17.4 us -> 0 us
  between operations: 13.7 us -> 0.02 us
    psum x1 -> x0, waiting for transfers between devices: 108 us -> none  [body(): gram = lax.psum(local_gram, ('grp', 'lane'))]
    pallas_call x0 -> x1, Pallas kernels: none -> 73.1 us  [body(): pl.pallas_call(functools.partial(kernel, groups, lanes), out_shape=jax.Sh...]
    scatter x3 -> x0, local copies, waits for them, and re-layouts: 27.4 us -> none  [the longest x1 11.6 us: place_rows(): return empty.at[flat_slots].set(received, mode='drop')]
    another operation x7 -> x0, other arithmetic: 24.2 us -> none  [the longest x3 12.4 us: body(): factor = jnp.linalg.cholesky(gram)]
    gather x9 -> x0, local copies, waits for them, and re-layouts: 17.5 us -> none  [the longest x3 8.6 us: operate(): blocks = extended[tile_cols]]
    ppermute x6 -> x0, starting transfers between devices: 15.9 us -> none  [from_behind(): lax.ppermute(value, axis, [(i, (i + by) % devices) for i in range(devices)])]
    dot_general x4 -> x0, matrix products: 15.2 us -> none  [the longest x3 12.8 us: operate(): jnp.einsum('bkij,bkjf->bif', tiles, blocks, preferred_element_type=jnp.fl...]
    all_to_all x2 -> x0, starting transfers between devices: 7.06 us -> none  [the longest x1 3.83 us: body(): lax.all_to_all(raw_buffer, 'lane', split_axis=0, concat_axis=0, tiled=True)]
  transfers between devices with their start and end apart: 9 -> 0, of which waited for: 5 -> 0; matrix products, arithmetic and copies ran while one was open for 26% -> 0% of each run, Pallas kernels for 0% -> 0%
where the time goes in v1:
time: 79.5 us; the launch traced here: 79.1 us
  Pallas kernels  73.1 us (92%)
  local copies, waits for them, and re-layouts  6.01 us (8%)
    pallas_call x1, Pallas kernels, body(): pl.pallas_call(functools.partial(kernel, groups, lanes), out_shape=jax.Sh...  73.1 us
    unnamed x14, local copies, waits for them, and re-layouts  6.01 us

profile of v1, /device:TPU:0, one launch (start us, length us, event | category | flops | bytes accessed | tf_op | source)
XLA Modules:
  0.0 79.1 jit_solution(1293717937959638785)
XLA Ops:
  0.0 0.8 copy.9.cols
  0.8 0.0 copy-start
  0.8 1.0 %copy-done = bf16[2048,128]{1,0:T(8,128)(2,1)S(1)} copy-done((bf16[2048,128]{1,0:T(8,128)(2,1)S(1)}, bf16[2048,128]{1,0:T(8,128)(2,1)}, u32[]{:S(2)}) %copy-start) | copy-done | bytes 524312
  1.8 0.0 copy-start.1
  1.8 0.7 copy-done.1
  2.5 0.0 copy-start.2
  2.5 0.7 copy-done.2
  3.2 0.0 copy-start.3
  3.2 0.7 copy-done.3
  3.9 0.0 copy-start.4
  3.9 0.7 copy-done.4
  4.6 0.0 copy-start.5
  4.6 0.7 copy-done.5
  5.2 73.1 %shard_map.82 = bf16[2048,128]{1,0:T(8,128)(2,1)S(1)} custom-call(s32[16,7]{1,0:T(8,128)S(1)} %copy.9.cols, s32[1,2]{1,0:T(1,128)S(1)} %copy-done.5, bf16[16,128,128]{2,1,0:T(8,128)(2,1)S(1)} %bitcast.4, bf16[16,7,128,128]{3,2,1,0:T(8,128)(2,1)} %tiles.1, s32[2,512]{1,0:T(2,128)S(1)} %bitcast.7, f32[4,128]{1,0:T(4,128)S(1)} %copy-done.4, ...), custom_call_target="tpu_custom_call" | custom-call | tf_op jit(solution)/shard_map/pallas_call | solution.py:289
  78.3 0.8 %copy.11 = bf16[2048,128]{1,0:T(8,128)(2,1)} copy(bf16[2048,128]{1,0:T(8,128)(2,1)S(1)} %shard_map.82) | data formatting | bytes 1048576
Async XLA Ops:
  0.8 1.0 %copy-start = (bf16[2048,128]{1,0:T(8,128)(2,1)S(1)}, bf16[2048,128]{1,0:T(8,128)(2,1)}, u32[]{:S(2)}) copy-start(bf16[2048,128]{1,0:T(8,128)(2,1)} %param.8) | copy-start | bytes 1572868
  1.8 0.7 copy-start.1
  2.5 0.7 copy-start.2
  3.2 0.7 copy-start.3
  3.9 0.7 copy-start.4
  4.6 0.7 copy-start.5

commit v2 on v1

--- a/solution.py
+++ b/solution.py
@@ -48,7 +48,8 @@
 
 
 def kernel(
-    groups, lanes, cols, counts, feats, tiles, index, coef, dest_lane, dest_slot, out,
+    groups, lanes, cols_h, counts_h, feats, tiles, index_h, coef_h, dest_lane_h, dest_slot_h, out,
+    cols, counts, index, coef, dest_lane, dest_slot, ready,
     ext0, ext1, ext2, tile_v, pick, snd, mixed, low, gat, codes, part, rs_buf, lane_buf, chunk, tot, placed,
     load_sem, halo_s, halo_r, code_s, code_r, rs_s, rs_r, ln_s, ln_r, ag_s, ag_r, x_s, x_r, f_s, f_r,
 ):
@@ -57,7 +58,7 @@
     rows = own_blocks * tile
     ext = (ext0, ext1, ext2)
     per_block = tiles.shape[1]
-    bnd = index.shape[1]
+    bnd = index_h.shape[1]
     lists = bnd // tile
     node_total = rows * groups * lanes
     half = lanes // 2
@@ -71,8 +72,21 @@
 
     load_tiles = pltpu.make_async_copy(tiles, tile_v, load_sem.at[0])
     load_feats = pltpu.make_async_copy(feats, ext[0].at[pl.ds(0, own_blocks)], load_sem.at[1])
+    small = [
+        pltpu.make_async_copy(src, dst, load_sem.at[2 + i])
+        for i, (src, dst) in enumerate(
+            [
+                (index_h, index), (counts_h, counts), (dest_lane_h, dest_lane),
+                (dest_slot_h, dest_slot), (cols_h, cols), (coef_h, coef),
+            ]
+        )
+    ]
+    for copy in small[:4]:
+        copy.start()
     load_feats.start()
     load_tiles.start()
+    for copy in small[4:]:
+        copy.start()
 
     barrier = pltpu.get_barrier_semaphore()
     for t in range(1, groups):
@@ -80,6 +94,8 @@
     for t in range(1, lanes):
         pl.semaphore_signal(barrier, inc=1, device_id=lane_at(t), device_id_type=MESH)
 
+    for copy in small[:4]:
+        copy.wait()
     codes[0] = dest_lane[...] * rows + dest_slot[...]
 
     row_pos = lax.broadcasted_iota(jnp.int32, (tile, tile), 0)
@@ -124,6 +140,34 @@
             copies.append(copy)
         return copies
 
+    tall = 256
+
+    def selector(code_slot, c):
+        target = lax.broadcasted_iota(jnp.int32, (tall, tile), 0) + (c * tall + l * rows)
+        return jnp.concatenate(
+            [onehot(codes[code_slot, r : r + 1, :] == target) for r in range(rows // tile)], axis=1
+        )
+
+    def prepare(code_slot, slot):
+        def step(c, _):
+            ready[slot, pl.ds(pl.multiple_of(c * tall, tall), tall)] = selector(code_slot, c)
+            return 0
+
+        lax.fori_loop(0, rows // tall, step, 0)
+
+    def place(gat_slot, code_slot, first=False, slot=None):
+        def step(c, _):
+            at = pl.ds(pl.multiple_of(c * tall, tall), tall)
+            chosen = selector(code_slot, c) if slot is None else ready[slot, at]
+            value = jnp.dot(chosen, gat[gat_slot], preferred_element_type=F32).astype(BF)
+            placed[at] = value if first else placed[at] + value
+            return 0
+
+        lax.fori_loop(0, rows // tall, step, 0)
+
+    def passed_code(t):
+        return lax.rem(l - sibling + 2 * t + lanes, lanes)
+
     halo_copies = halo(0)
     code_copies = []
     for t in range(1, lanes):
@@ -131,6 +175,8 @@
         copy.start()
         code_copies.append(copy)
     load_tiles.wait()
+    for copy in small[4:]:
+        copy.wait()
 
     for k in range(1, ORDER + 1):
         for copy in halo_copies:
@@ -167,6 +213,13 @@
         lax.fori_loop(0, rows // tile, block, 0, unroll=4)
         if k < ORDER:
             halo_copies = halo(k)
+            if k == 1:
+                for copy in code_copies:
+                    copy.wait()
+                if half > 1:
+                    prepare(2, 0)
+            elif k == 2 and half > 1:
+                prepare(passed_code(1), 1)
 
     step = 512
     square = jnp.zeros((2 * width, 2 * width), F32)
@@ -190,26 +243,7 @@
         rs_copies.append(copy)
     sib_copies = [remote(gat.at[0], gat.at[half], f_s.at[0], f_r.at[0], (g, sibling))]
     sib_copies[0].start()
-    for copy in code_copies:
-        copy.wait()
-
-    def place(gat_slot, code_slot, first):
-        tall = 256
-
-        def body(c, _):
-            at = pl.ds(pl.multiple_of(c * tall, tall), tall)
-            target = lax.broadcasted_iota(jnp.int32, (tall, tile), 0) + (c * tall + l * rows)
-            selector = jnp.concatenate(
-                [onehot(codes[code_slot, r : r + 1, :] == target) for r in range(rows // tile)], axis=1
-            )
-            value = jnp.dot(selector, gat[gat_slot], preferred_element_type=F32).astype(BF)
-            if first:
-                placed[at] = value
-            else:
-                placed[at] = placed[at] + value
-            return 0
-
-        lax.fori_loop(0, rows // tall, body, 0)
+    place(0, 0, first=True)
 
     for copy in rs_copies:
         copy.wait()
@@ -239,7 +273,8 @@
         copy = remote(chunk, tot.at[t], ag_s.at[t], ag_r.at[t], grp_at(t))
         copy.start()
         ag_copies.append(copy)
-    place(0, 0, True)
+    sib_copies[0].wait()
+    place(half, passed_code(0))
     for copy in ag_copies:
         copy.wait()
     gram = jnp.concatenate(
@@ -255,10 +290,10 @@
         copy.start()
         sib_copies.append(copy)
     for t in range(1, half):
-        place(t, 2 * t, False)
-    for t in range(half):
+        place(t, 2 * t, slot=0 if t == 1 else None)
+    for t in range(1, half):
         sib_copies[t].wait()
-        place(half + t, lax.rem(l - sibling + 2 * t + lanes, lanes), False)
+        place(half + t, passed_code(t), slot=1 if t == 1 else None)
 
     radius = math.sqrt(width)
 
@@ -284,14 +319,20 @@
     share = width // groups
     dma = pltpu.SemaphoreType.DMA
     vmem = pl.BlockSpec(memory_space=pltpu.VMEM)
-    smem = pl.BlockSpec(memory_space=pltpu.SMEM)
     hbm = pl.BlockSpec(memory_space=pl.ANY)
     return pl.pallas_call(
         functools.partial(kernel, groups, lanes),
         out_shape=jax.ShapeDtypeStruct((rows, width), BF),
-        in_specs=[smem, smem, hbm, hbm, vmem, vmem, vmem, vmem],
+        in_specs=[hbm] * 8,
         out_specs=vmem,
         scratch_shapes=[
+            pltpu.SMEM((blocks, per_block), jnp.int32),
+            pltpu.SMEM((1, 2), jnp.int32),
+            pltpu.VMEM((2, bnd), jnp.int32),
+            pltpu.VMEM((ORDER + 1, width), F32),
+            pltpu.VMEM((rows // 128, 128), jnp.int32),
+            pltpu.VMEM((rows // 128, 128), jnp.int32),
+            pltpu.VMEM((2, rows, rows), BF),
             *[pltpu.VMEM(((rows + 2 * bnd) // tile, tile, width), BF)] * ORDER,
             pltpu.VMEM((blocks, per_block, tile, tile), BF),
             pltpu.VMEM((2 * bnd, rows), BF),
@@ -306,7 +347,7 @@
             pltpu.VMEM((share, width), F32),
             pltpu.VMEM((groups, share, width), F32),
             pltpu.VMEM((rows, width), BF),
-            dma((2,)),
+            dma((8,)),
             dma((ORDER, 2)), dma((ORDER, 2)),
             dma((lanes,)), dma((lanes,)),
             dma((groups,)), dma((groups,)),

time: 79.5 us -> 74.7 us (0.940)
  Pallas kernels: 73.1 us -> 68.3 us
    pallas_call x1, Pallas kernels: 73.1 us -> 68.3 us  [body(): pl.pallas_call(functools.partial(kernel, groups, lanes), out_shape=jax.Sh...]
where the time goes in v2:
time: 74.7 us; the launch traced here: 74.3 us
  Pallas kernels  68.3 us (91%)
  local copies, waits for them, and re-layouts  6.01 us (8%)
    pallas_call x1, Pallas kernels, body(): pl.pallas_call(functools.partial(kernel, groups, lanes), out_shape=jax.Sh...  68.3 us
    unnamed x14, local copies, waits for them, and re-layouts  6.01 us

profile of v2, /device:TPU:0, one launch (start us, length us, event | category | flops | bytes accessed | tf_op | source)
XLA Modules:
  0.0 74.3 jit_solution(5627954603605311145)
XLA Ops:
  0.0 0.8 %copy.9.cols_h = s32[16,7]{1,0:T(8,128)S(1)} copy(s32[16,7]{0,1:T(8,128)} %param.10) | data formatting | bytes 896 | tf_op args[2]
  0.8 0.0 copy-start
  0.8 1.0 %copy-done = bf16[2048,128]{1,0:T(8,128)(2,1)S(1)} copy-done((bf16[2048,128]{1,0:T(8,128)(2,1)S(1)}, bf16[2048,128]{1,0:T(8,128)(2,1)}, u32[]{:S(2)}) %copy-start) | copy-done | bytes 524312
  1.8 0.0 copy-start.1
  1.8 0.7 copy-done.1
  2.5 0.0 copy-start.2
  2.5 0.7 copy-done.2
  3.2 0.0 copy-start.3
  3.2 0.7 copy-done.3
  3.9 0.0 copy-start.4
  3.9 0.7 copy-done.4
  4.6 0.0 copy-start.5
  4.6 0.7 copy-done.5
  5.2 68.3 %shard_map.82 = bf16[2048,128]{1,0:T(8,128)(2,1)S(1)} custom-call(s32[16,7]{1,0:T(8,128)S(1)} %copy.9.cols_h, s32[1,2]{1,0:T(1,128)S(1)} %copy-done.5, bf16[16,128,128]{2,1,0:T(8,128)(2,1)S(1)} %bitcast.4, bf16[16,7,128,128]{3,2,1,0:T(8,128)(2,1)} %tiles.1, s32[2,512]{1,0:T(2,128)S(1)} %bitcast.7, f32[4,128]{1,0:T(4,128)S(1)} %copy-done.4, ...), custom_call_target="tpu_custom_call" | custom-call | tf_op jit(solution)/shard_map/pallas_call | solution.py:323
  73.5 0.8 %copy.11 = bf16[2048,128]{1,0:T(8,128)(2,1)} copy(bf16[2048,128]{1,0:T(8,128)(2,1)S(1)} %shard_map.82) | data formatting | bytes 1048576
Async XLA Ops:
  0.8 1.0 %copy-start = (bf16[2048,128]{1,0:T(8,128)(2,1)S(1)}, bf16[2048,128]{1,0:T(8,128)(2,1)}, u32[]{:S(2)}) copy-start(bf16[2048,128]{1,0:T(8,128)(2,1)} %param.8) | copy-start | bytes 1572868
  1.8 0.7 copy-start.1
  2.5 0.7 copy-start.2
  3.2 0.7 copy-start.3
  3.9 0.7 copy-start.4
  4.6 0.7 copy-start.5
